TPU v7x, 256 devices: a whole 4x4x8 slice. The times are simulated.
256 devices in a mesh: row: 16 (over y_hi, x, core), col: 16 (over z, y_lo).
Axes of the slice: x: 4, y: 4 (y_hi: 2, y_lo: 2; y = y_hi * 2 + y_lo), z: 8, core: 2. Of those that a mesh axis runs over, the one named last changes fastest.
Arguments:
- attn_context: bfloat16 [8192, 4096], P('row', 'col'), may hold values from -6 to 6
- residual: bfloat16 [8192, 2048], P('row', 'col'), may hold values from -8 to 8
- w_out: bfloat16 [4096, 2048], P('col'), may hold values from -0.09375 to 0.09375
- gain_post: bfloat16 [2048], replicated, may hold values from 0.5 to 1.5
- gain_input: bfloat16 [2048], replicated, may hold values from 0.5 to 1.5
- routes: int32 [8192, 8], P('row'), may hold values from 0 to 127, all different within a row; in each aligned block of 512 rows (0 to 511, 512 to 1023, ...) at most 64 rows name the same one
- router_scores: float32 [8192, 8], P('row'), may hold values from 0.02 to 1
- w_gate: bfloat16 [256, 2048, 384], P(('row', 'col')), may hold values from -0.125 to 0.125
- w_up: bfloat16 [256, 2048, 384], P(('row', 'col')), may hold values from -0.125 to 0.125
- w_down: bfloat16 [256, 384, 2048], P(('row', 'col')), may hold values from -0.21875 to 0.21875
- w_query: bfloat16 [2048, 4096], P(None, 'col'), may hold values from -1 to 1
- w_keyval: bfloat16 [2048, 1024], P(None, 'col'), may hold values from -1 to 1
- segment_ids: int32 [16, 504], P('row'), may hold values from 0 to 3, never falling along the last dimension, each value on 1 to 252 neighbouring positions
- cache_lengths: int32 [128], P('row'), may hold values from 1 to 1024, 65536 in all
- holders: int32 [128], P('row'), may hold values from 0 to 127, each once
- cache_keys: bfloat16 [128, 1024, 512], P('row', 'col'), may hold values from -12 to 12
- cache_values: bfloat16 [128, 1024, 512], P('row', 'col'), may hold values from -12 to 12
Outputs:
- hidden_out: bfloat16 [8192, 2048], P('row', 'col')
- new_cache: bfloat16 [8192, 1024], P('row', 'col')
- attention_out: bfloat16 [8192, 4096], P('row', 'col')
Inputs may be any that keep to these rules, and one draw needn't show every extreme that they name: `routes`: in the 512 rows of one index of row, no expert is named by more than 64 rows, and in every draw some expert is named by exactly 64. `segment_ids`: each prompt has at most 252 rows and one has exactly that many. `cache_lengths`: the lengths sum to 65536 and the largest is 1024. `holders`: each cache entry belongs to exactly one decode row.
All inputs are finite; a program needn't handle non-finite values. No bound on the sum of `cache_lengths` on one device may be relied on, other than what follows from the above.
Results may differ from a plain program's by a relative error of at most 0.0175.
Values may be sent and summed in bfloat16 or wider, within the bound.
A program may use at most 128 MiB of HBM per device.

v0:
```python
import jax
import jax.numpy as jnp
from jax import lax
from jax.sharding import PartitionSpec as P

TOP = 8
QH = 32
KVH = 4
HD = 128
EPSILON = 1e-06
ROPE_THETA = 1000000.0
NEGATIVE = -1e30


def merged_2(value, axis, join):
    pieces = jax.tree.map(lambda part: lax.all_gather(part, axis), value)
    head = jax.tree.map(lambda part: part[0], pieces)
    tail = jax.tree.map(lambda part: part[1:], pieces)
    running, _ = lax.scan(lambda running, share: (join(running, share), None), head, tail)
    return running


def rms_norm(hidden, gain_vector):
    values = hidden.astype(jnp.float32)
    inverse = lax.rsqrt(jnp.mean(values * values, axis=-1, keepdims=True) + EPSILON)
    return (values * inverse * gain_vector.astype(jnp.float32)).astype(jnp.bfloat16)


def rotate(values, positions):
    head_width = values.shape[-1]
    half_width = head_width // 2
    indices = jnp.arange(half_width).astype(jnp.float32)
    inverse = ROPE_THETA ** (-2.0 * indices / head_width)
    angles = positions.astype(jnp.float32)[:, None] * inverse[None, :]
    cosine = jnp.concatenate([jnp.cos(angles), jnp.cos(angles)], axis=-1)[:, None, :]
    sine_part = jnp.concatenate([jnp.sin(angles), jnp.sin(angles)], axis=-1)[:, None, :]
    floats = values.astype(jnp.float32)
    turned = jnp.concatenate([-floats[..., half_width:], floats[..., :half_width]], axis=-1)
    return (floats * cosine + turned * sine_part).astype(jnp.bfloat16)


def segment_positions(segment_rows):
    earlier = jnp.sum((segment_rows[None, :] < segment_rows[:, None]).astype(jnp.int32), axis=1)
    return jnp.arange(segment_rows.shape[0], dtype=jnp.int32) - earlier


def spread_norm(hidden, gain_vector):
    gathered = lax.all_gather(hidden, "col", axis=1, tiled=True)
    return (gathered, rms_norm(gathered, gain_vector))


def join_partials(first, second):
    highest = jnp.maximum(first[0], second[0])
    factor_one = jnp.exp(first[0] - highest)
    factor_two = jnp.exp(second[0] - highest)
    weight_mass = first[1] * factor_one + second[1] * factor_two
    accum_out = first[2] * factor_one[..., None] + second[2] * factor_two[..., None]
    return (highest, weight_mass, accum_out)


def shards(
    attn_context,
    residual,
    w_out,
    gain_post,
    gain_input,
    routes,
    router_scores,
    w_gate,
    w_up,
    w_down,
    w_query,
    w_keyval,
    segment_ids,
    cache_lengths,
    holders,
    cache_keys,
    cache_values,
):
    col_index = lax.axis_index("col")
    col_count = lax.axis_size("col")
    row_count = lax.axis_size("row")
    tok_rows = attn_context.shape[0]
    share_width = residual.shape[1]
    model_width = share_width * col_count
    projected = jnp.dot(attn_context, w_out, preferred_element_type=jnp.float32)
    summed = lax.psum_scatter(projected, "col", scatter_dimension=1, tiled=True)
    hidden_mid = (residual.astype(jnp.float32) + summed).astype(jnp.bfloat16)
    full_mid, normed = spread_norm(hidden_mid, gain_post)
    group_width = col_count // 2
    expert_count = row_count * group_width
    capacity = 2 * tok_rows * TOP // expert_count
    route_weight = router_scores / jnp.sum(router_scores, axis=1, keepdims=True)
    matching = routes % group_width == col_index // 2
    target = routes // group_width
    dest_ids = jnp.arange(row_count, dtype=jnp.int32)
    hitting = matching[:, :, None] & (target[:, :, None] == dest_ids[None, None, :])
    sent_flag = jnp.sum(hitting.astype(jnp.int32), axis=1)
    sent_weight = jnp.sum(jnp.where(hitting, route_weight[:, :, None], 0.0), axis=1)
    place = jnp.cumsum(sent_flag, axis=0) - sent_flag
    dest_or_drop = jnp.where(sent_flag > 0, dest_ids[None, :], row_count)
    row_ids = jnp.broadcast_to(
        jnp.arange(tok_rows, dtype=jnp.int32)[:, None], (tok_rows, row_count)
    )
    slot_rows = (
        jnp.full((row_count, capacity), tok_rows, jnp.int32)
        .at[dest_or_drop, place]
        .set(row_ids, mode="drop")
    )
    slot_weight = (
        jnp.zeros((row_count, capacity), jnp.float32)
        .at[dest_or_drop, place]
        .set(sent_weight, mode="drop")
    )
    padded = jnp.concatenate([normed, jnp.zeros((1, model_width), jnp.bfloat16)], axis=0)
    outgoing = padded[slot_rows]
    gate_local = w_gate[0]
    up_local = w_up[0]
    down_local = w_down[0]
    arrived = lax.all_to_all(outgoing, "row", split_axis=0, concat_axis=0, tiled=True)
    flat_rows = arrived.reshape(-1, arrived.shape[2])
    gate_part = jnp.dot(flat_rows, gate_local, preferred_element_type=jnp.float32)
    up_part = jnp.dot(flat_rows, up_local, preferred_element_type=jnp.float32)
    inner = (jax.nn.silu(gate_part) * up_part).astype(jnp.bfloat16)
    result = jnp.dot(inner, down_local, preferred_element_type=jnp.float32).astype(jnp.bfloat16)
    returned = lax.all_to_all(
        result.reshape(arrived.shape), "row", split_axis=0, concat_axis=0, tiled=True
    )
    weighted = slot_weight[:, :, None] * returned.astype(jnp.float32)
    partial_moe = (
        jnp.zeros((tok_rows, model_width), jnp.float32)
        .at[slot_rows.reshape(-1)]
        .add(weighted.reshape(-1, model_width), mode="drop")
    )
    moe_share = lax.psum_scatter(partial_moe, "col", scatter_dimension=1, tiled=True)
    hidden_out = (hidden_mid.astype(jnp.float32) + moe_share).astype(jnp.bfloat16)
    _, x_in = spread_norm(hidden_out, gain_input)
    heads_local = QH // col_count
    dec_count = cache_lengths.shape[0]
    score_scale = HD ** (-0.5)
    query_local = (
        jnp.dot(x_in, w_query, preferred_element_type=jnp.float32)
        .astype(jnp.bfloat16)
        .reshape(tok_rows, heads_local, HD)
    )
    keyval_local = jnp.dot(x_in, w_keyval, preferred_element_type=jnp.float32).astype(jnp.bfloat16)
    position = jnp.concatenate([cache_lengths, segment_positions(segment_ids[0])], axis=0)
    query_rot = rotate(query_local, position)
    dec_query = query_rot[:dec_count].reshape(dec_count, heads_local * HD)
    keyval_all, payload = (
        lax.all_gather(keyval_local, "col", axis=1, tiled=True),
        lax.all_gather(dec_query, "col", axis=1, tiled=True),
    )
    keyval_heads = keyval_all.reshape(tok_rows, KVH, 2, HD)
    key_rot = rotate(keyval_heads[:, :, 0, :], position)
    value_rows = keyval_heads[:, :, 1, :]
    cache_full = jnp.stack([key_rot, value_rows], axis=2).reshape(tok_rows, 2 * KVH * HD)
    cache_share = cache_full.shape[1] // col_count
    new_cache = lax.dynamic_slice_in_dim(cache_full, col_index * cache_share, cache_share, 1)
    head_kv = col_index * heads_local // (QH // KVH)
    my_keys = lax.dynamic_index_in_dim(key_rot, head_kv, 1, keepdims=False)
    my_values = lax.dynamic_index_in_dim(value_rows, head_kv, 1, keepdims=False)
    prompt_query = query_rot[dec_count:]
    prompt_keys = my_keys[dec_count:]
    prompt_values = my_values[dec_count:]
    prompt_rows = prompt_query.shape[0]
    scores = (
        jnp.einsum("ihd,jd->hij", prompt_query, prompt_keys, preferred_element_type=jnp.float32)
        * score_scale
    )
    ordinal = jnp.arange(prompt_rows)
    segment_rows = segment_ids[0]
    allowed = (segment_rows[:, None] == segment_rows[None, :]) & (
        ordinal[None, :] <= ordinal[:, None]
    )
    scores = jnp.where(allowed[None, :, :], scores, NEGATIVE)
    highest = jnp.max(scores, axis=-1, keepdims=True)
    exponent = jnp.exp(scores - highest)
    probability = (exponent / jnp.sum(exponent, axis=-1, keepdims=True)).astype(jnp.bfloat16)
    prompt_out = jnp.einsum(
        "hij,jd->ihd", probability, prompt_values, preferred_element_type=jnp.float32
    )
    prompt_out = prompt_out.astype(jnp.bfloat16).reshape(prompt_rows, heads_local * HD)
    holder_dev = holders // dec_count
    holder_slot = holders % dec_count
    outbox = (
        jnp.zeros((row_count, dec_count, payload.shape[1]), jnp.bfloat16)
        .at[holder_dev, holder_slot]
        .set(payload)
    )
    length_box = (
        jnp.zeros((row_count, dec_count), jnp.int32).at[holder_dev, holder_slot].set(cache_lengths)
    )
    inbox, length_in = (
        lax.all_to_all(outbox, "row", split_axis=0, concat_axis=0, tiled=True),
        lax.all_to_all(length_box, "row", split_axis=0, concat_axis=0, tiled=True),
    )
    slot_query = jnp.sum(inbox.astype(jnp.float32), axis=0).astype(jnp.bfloat16)
    slot_length = jnp.sum(length_in, axis=0)
    span_len = cache_keys.shape[1]
    span_start = col_index * span_len
    grouped = slot_query.reshape(dec_count, KVH, QH // KVH, HD)
    held_keys = cache_keys.reshape(dec_count, span_len, KVH, HD)
    held_values = cache_values.reshape(dec_count, span_len, KVH, HD).astype(jnp.float32)
    held_scores = (
        jnp.einsum("sgqd,stgd->sgqt", grouped, held_keys, preferred_element_type=jnp.float32)
        * score_scale
    )
    valid = ((span_start + jnp.arange(span_len))[None, :] < slot_length[:, None])[:, None, None, :]
    held_scores = jnp.where(valid, held_scores, NEGATIVE)
    score_top = jnp.max(held_scores, axis=-1)
    held_exp = jnp.where(valid, jnp.exp(held_scores - score_top[..., None]), 0.0)
    weight_mass = jnp.sum(held_exp, axis=-1).reshape(dec_count, QH)
    accum_out = jnp.einsum(
        "sgqt,stgd->sgqd", held_exp, held_values, precision=lax.Precision.HIGHEST
    ).reshape(dec_count, QH, HD)
    score_top = score_top.reshape(dec_count, QH)
    merged = merged_2((score_top, weight_mass, accum_out), "col", join_partials)
    part_top = lax.dynamic_slice_in_dim(merged[0], col_index * heads_local, heads_local, 1)
    part_mass = lax.dynamic_slice_in_dim(merged[1], col_index * heads_local, heads_local, 1)
    part_accum = lax.dynamic_slice_in_dim(merged[2], col_index * heads_local, heads_local, 1)
    reply_top = jnp.broadcast_to(part_top[None], (row_count,) + part_top.shape)
    reply_mass = jnp.broadcast_to(part_mass[None], (row_count,) + part_mass.shape)
    reply_accum = jnp.broadcast_to(part_accum[None], (row_count,) + part_accum.shape)
    back_top, back_mass, back_accum = (
        lax.all_to_all(reply_top, "row", split_axis=0, concat_axis=0, tiled=True),
        lax.all_to_all(reply_mass, "row", split_axis=0, concat_axis=0, tiled=True),
        lax.all_to_all(reply_accum, "row", split_axis=0, concat_axis=0, tiled=True),
    )
    remote_top = back_top[holder_dev, holder_slot]
    remote_mass = back_mass[holder_dev, holder_slot]
    remote_accum = back_accum[holder_dev, holder_slot]
    own_query = query_rot[:dec_count].astype(jnp.float32)
    own_key = my_keys[:dec_count].astype(jnp.float32)
    own_value = my_values[:dec_count].astype(jnp.float32)
    own_score = (
        jnp.einsum("shd,sd->sh", own_query, own_key, precision=lax.Precision.HIGHEST) * score_scale
    )
    final_top = jnp.maximum(remote_top, own_score)
    remote_factor = jnp.exp(remote_top - final_top)
    own_factor = jnp.exp(own_score - final_top)
    numerator = (
        remote_accum * remote_factor[..., None] + own_factor[..., None] * own_value[:, None, :]
    )
    denominator = remote_mass * remote_factor + own_factor
    decode_out = (
        (numerator / denominator[..., None])
        .reshape(dec_count, heads_local * HD)
        .astype(jnp.bfloat16)
    )
    attention_out = jnp.concatenate([decode_out, prompt_out], axis=0)
    return (hidden_out, new_cache, attention_out)


def solution(mesh):
    return jax.shard_map(
        shards,
        mesh=mesh,
        in_specs=(
            P("row", "col"),
            P("row", "col"),
            P("col", None),
            P(),
            P(),
            P("row", None),
            P("row", None),
            P(("row", "col"), None, None),
            P(("row", "col"), None, None),
            P(("row", "col"), None, None),
            P(None, "col"),
            P(None, "col"),
            P("row", None),
            P("row"),
            P("row"),
            P("row", "col", None),
            P("row", "col", None),
        ),
        out_specs=(P("row", "col"), P("row", "col"), P("row", "col")),
        check_vma=False,
    )
```

profile of v0, /device:TPU:1, one launch (start us, length us, event | category | flops | bytes accessed | tf_op | source)
XLA Modules:
  0.0 781.5 jit_solution(6182529554980959249)
XLA Ops:
  7.2 4.1 fusion.103
  11.4 102.1 %reduce-scatter.3.cloned.1.call-done = f32[512,128]{1,0:T(8,128)} async-done(((f32[512,2048]{1,0:T(8,128)}), f32[512,128]{1,0:T(8,128)}) %reduce-scatter.3.cloned.1.call-update) | async-done | bytes 262160 | tf_op jit(solution)/shard_map/reduce_scatter | solution.py:87
  113.5 1.6 add_convert_fusion.1
  115.3 1.2 reduce-window.6
  117.4 30.4 %scatter_custom_fusion.3 = s32[1024]{0:T(1024)S(1)} fusion(s32[8192]{0:T(1024)S(1)} %reshape.353, s32[8192]{0:T(1024)S(1)} %reshape.355, s32[]{:T(128)} %constant.121.clone.1), kind=kCustom, calls=%fused_computation.150 | custom fusion | bytes 4100
  148.0 42.8 %all-gather.5.cloned.1.call-done = bf16[512,2048]{1,0:T(8,128)(2,1)} async-done(((bf16[512,128]{1,0:T(8,128)(2,1)}), bf16[512,2048]{1,0:T(8,128)(2,1)}) %all-gather.5.cloned.1.call-update) | async-done | bytes 2097168 | tf_op jit(solution)/shard_map/all_gather | solution.py:48
  190.8 2.2 fusion.4
  193.6 1.5 concatenate.52
  195.0 10.7 %gather_fusion = bf16[1024,2048]{1,0:T(8,128)(2,1)} fusion(bf16[513,2048]{1,0:T(8,128)(2,1)} %concatenate.52, s32[1024]{0:T(1024)S(1)} %broadcast_clamp_fusion), kind=kCustom, calls=%fused_computation | custom fusion | bytes 8392704 | tf_op jit(solution)/shard_map/gather | solution.py:116
  205.7 68.1 %all_to_all.39 = bf16[16,64,2048]{2,1,0:T(8,128)(2,1)S(1)} all-to-all(bf16[16,64,2048]{2,1,0:T(8,128)(2,1)} %bitcast.177), channel_id=1, replica_groups=mesh['row'=16,'col'=16] {'row'}, dimensions={0} | all-to-all | bytes 8388608 | tf_op jit(solution)/shard_map/all_to_all | solution.py:120
  273.9 2.0 copy-done.3
  275.9 3.6 fusion.16
  279.4 7.8 convolution_convert_fusion
  287.2 5.5 all-to-all-start.1
  293.2 30.6 %scatter_custom_fusion.4 = f32[1024]{0:T(1024)S(1)} fusion(s32[8192]{0:T(1024)S(1)} %reshape.353, f32[8192]{0:T(1024)S(1)} %reshape.361, f32[]{:T(128)} %constant.120.clone.1), kind=kCustom, calls=%fused_computation.148 | custom fusion | bytes 4100
  323.9 24.7 %all-to-all-done.1 = bf16[16,64,2048]{2,1,0:T(8,128)(2,1)} async-done(((bf16[16,64,2048]{2,1,0:T(8,128)(2,1)}), bf16[16,64,2048]{2,1,0:T(8,128)(2,1)}, u32[]{:S(2)}, u32[]{:S(2)}) %all-to-all-start.1) | async-done | bytes 4194336 | tf_op jit(solution)/shard_map/all_to_all | solution.py:126
  348.5 6.0 convert_multiply_fusion
  354.5 16.9 %scatter_custom_fusion = f32[512,2048]{1,0:T(8,128)} fusion(s32[1024]{0:T(1024)S(1)} %bitcast.191, f32[1024,2048]{1,0:T(8,128)} %bitcast.178, f32[]{:T(128)} %constant.120.clone.1), kind=kCustom, calls=%fused_computation.30 | custom fusion | flops 2097152 | bytes 4194816 | tf_op jit(solution)/shard_map/scatter-add | solution.py:133
  371.5 98.3 %reduce-scatter.5.cloned.1.call-done = f32[512,128]{1,0:T(8,128)} async-done(((f32[512,2048]{1,0:T(8,128)}), f32[512,128]{1,0:T(8,128)}) %reduce-scatter.5.cloned.1.call-update) | async-done | bytes 262160 | tf_op jit(solution)/shard_map/reduce_scatter | solution.py:135
  469.8 1.6 add_convert_fusion
  473.1 9.1 %all-to-all-start.2 = ((s32[16,1,8]{2,1,0:T(1,128)}), s32[16,1,8]{2,1,0:T(1,128)S(1)}, u32[]{:S(2)}, u32[]{:S(2)}) async-start(s32[16,1,8]{2,1,0:T(1,128)} %copy.82), calls=%async_computation.4 | async-start | bytes 16384 | tf_op jit(solution)/shard_map/all_to_all | solution.py:196
  483.9 63.3 %all-gather.7.cloned.1.call-done = bf16[512,2048]{1,0:T(8,128)(2,1)} async-done(((bf16[512,128]{1,0:T(8,128)(2,1)}), bf16[512,2048]{1,0:T(8,128)(2,1)}) %all-gather.7.cloned.1.call-update) | async-done | bytes 2097168 | tf_op jit(solution)/shard_map/all_gather | solution.py:48
  547.2 2.2 fusion.7
  549.5 1.5 convolution_convert_fusion.3
  551.0 2.5 convolution_convert_fusion.1
  554.2 24.0 %all_gather.24 = bf16[8,4096]{1,0:T(8,128)(2,1)S(1)} all-gather(bf16[8,256]{1,0:T(8,128)(2,1)S(1)} %get-tuple-element.84), channel_id=1, replica_groups=mesh['row'=16,'col'=16] {'col'}, dimensions={1}, use_global_device_ids=true | all-gather | bytes 69632 | tf_op jit(solution)/shard_map/all_gather | solution.py:152
  578.1 1.1 broadcast_in_dim.96
  579.2 3.3 scatter_fusion.1
  582.6 25.2 %all-to-all-start.3 = ((bf16[16,8,4096]{2,1,0:T(8,128)(2,1)}), bf16[16,8,4096]{2,1,0:T(8,128)(2,1)S(1)}, u32[]{:S(2)}, u32[]{:S(2)}) async-start(bf16[16,8,4096]{2,1,0:T(8,128)(2,1)} %scatter_fusion.1), calls=%async_computation.5 | async-start | bytes 2097152 | tf_op jit(solution)/shard_map/all_to_all | solution.py:195
  607.9 18.1 %all-to-all-done.3 = bf16[16,8,4096]{2,1,0:T(8,128)(2,1)S(1)} async-done(((bf16[16,8,4096]{2,1,0:T(8,128)(2,1)}), bf16[16,8,4096]{2,1,0:T(8,128)(2,1)S(1)}, u32[]{:S(2)}, u32[]{:S(2)}) %all-to-all-start.3) | async-done | bytes 1048608 | tf_op jit(solution)/shard_map/all_to_all | solution.py:195
  626.6 1.2 convolution_bitcast_fusion
  629.2 23.4 %all_gather.26 = f32[16,8,32]{2,1,0:T(8,128)S(1)} all-gather(f32[1,8,32]{2,1,0:T(8,128)S(1)} %all_gather_reshape.10), channel_id=1, replica_groups=mesh['row'=16,'col'=16] {'col'}, dimensions={0}, use_global_device_ids=true | all-gather | bytes 17408 | tf_op jit(solution)/shard_map/all_gather | solution.py:16
  652.7 27.2 %all_gather.25 = f32[16,8,32]{2,1,0:T(8,128)S(1)} all-gather(f32[1,8,32]{2,1,0:T(8,128)S(1)} %all_gather_reshape.9), channel_id=1, replica_groups=mesh['row'=16,'col'=16] {'col'}, dimensions={0}, use_global_device_ids=true | all-gather | bytes 17408 | tf_op jit(solution)/shard_map/all_gather | solution.py:16
  679.8 1.3 fusion.97
  682.5 1.4 fusion.96
  684.1 2.5 fusion.99
  686.6 3.1 fusion.20
  689.7 1.1 copy.94
  693.9 10.1 %all-gather.11.cloned.1.call-done = f32[16,8,32,128]{3,2,1,0:T(8,128)} async-done(((f32[1,8,32,128]{3,2,1,0:T(8,128)}), f32[16,8,32,128]{3,2,1,0:T(8,128)}) %all-gather.11.cloned.1.call-update) | async-done | bytes 2097168 | tf_op jit(solution)/shard_map/all_gather | solution.py:16
  704.0 3.0 slice.119
  708.0 16.8 %while.14 = (s32[]{:T(128)}, f32[8,32]{1,0:T(8,128)S(1)}, f32[8,32]{1,0:T(8,128)S(1)}, f32[8,32,128]{2,1,0:T(8,128)S(1)}, f32[15,8,32]{2,1,0:T(8,128)S(1)}, /*in...) while((s32[]{:T(128)}, f32[8,32]{1,0:T(8,128)S(1)}, f32[8,32]{1,0:T(8,128)S(1)}, ...), condition=%wide.region_20.21_spmd, body=%wide.region_19.20_spmd.sunk | while | flops 99842 | bytes 403549 | solution.py:19
  708.0 1.2 fusion.116
  725.6 16.2 %all-to-all-start.5 = ((f32[16,8,2]{1,2,0:T(2,128)}), f32[16,8,2]{1,2,0:T(2,128)S(1)}, u32[]{:S(2)}, u32[]{:S(2)}) async-start(f32[16,8,2]{1,2,0:T(2,128)} %broadcast_in_dim.100), calls=%async_computation.7 | async-start | bytes 32768 | tf_op jit(solution)/shard_map/all_to_all | solution.py:226
  742.0 7.1 all-to-all-done.5
  749.7 3.7 all-to-all-start.6
  754.2 6.6 all-to-all-done.6
  761.5 3.7 all-to-all-start.4
  765.9 6.9 all-to-all-done.4
  (185 shorter events, 34.6 us)
Async XLA Ops:
  7.2 272.2 %copy-start = (bf16[1,384,2048]{2,1,0:T(8,128)(2,1)S(1)}, bf16[1,384,2048]{2,1,0:T(8,128)(2,1)}, u32[]{:S(2)}) copy-start(bf16[1,384,2048]{2,1,0:T(8,128)(2,1)} %param.28) | copy-start | bytes 4718596
  7.2 106.3 %reduce-scatter.3.cloned.1.call-start = ((), (), s32[]{:S(2)}) async-start(), calls=%async_computation.9 | async-start | bytes 4456448 | tf_op jit(solution)/shard_map/reduce_scatter | solution.py:87
  11.3 102.2 %copy-start.11 = (bf16[512,128]{1,0:T(8,128)(2,1)S(1)}, bf16[512,128]{1,0:T(8,128)(2,1)}, u32[]{:S(2)}) copy-start(bf16[512,128]{1,0:T(8,128)(2,1)} %param.20) | copy-start | bytes 393220
  11.3 103.8 %copy-start.12 = (s32[512,8]{0,1:T(8,128)S(1)}, s32[512,8]{0,1:T(8,128)}, u32[]{:S(2)}) copy-start(s32[512,8]{0,1:T(8,128)} %param.24) | copy-start | bytes 49156
  11.3 105.5 %copy-start.19 = (s32[2]{0:T(128)S(1)}, s32[2]{0:T(128)}, u32[]{:S(2)}) copy-start(s32[2]{0:T(128)} %constant.155) | copy-start | bytes 28
  11.3 105.6 %copy-start.18 = (s32[2]{0:T(128)S(1)}, s32[2]{0:T(128)}, u32[]{:S(2)}) copy-start(s32[2]{0:T(128)} %constant.158) | copy-start | bytes 28
  11.3 136.7 %copy-start.15 = (bf16[2048]{0:T(1024)(128)(2,1)S(1)}, bf16[2048]{0:T(1024)(128)(2,1)}, u32[]{:S(2)}) copy-start(bf16[2048]{0:T(1024)(128)(2,1)} %param.22) | copy-start | bytes 12292
  11.3 179.4 %all-gather.5.cloned.1.call-start = ((), (), s32[]{:S(2)}) async-start(), calls=%async_computation.10 | async-start | bytes 2228224 | tf_op jit(solution)/shard_map/all_gather | solution.py:48
  190.8 2.2 copy-start.2
  205.7 70.1 %copy-start.20 = (bf16[1,2048,384]{2,1,0:T(8,128)(2,1)S(1)}, bf16[1,2048,384]{2,1,0:T(8,128)(2,1)}, u32[]{:S(2)}) copy-start(bf16[1,2048,384]{2,1,0:T(8,128)(2,1)} %param.26) | copy-start | bytes 4718596
  273.9 2.0 copy-start.3
  275.8 3.6 copy-start.21
  287.2 5.6 copy-start.13
  287.2 61.3 %all-to-all-start.1 = ((bf16[16,64,2048]{2,1,0:T(8,128)(2,1)}), bf16[16,64,2048]{2,1,0:T(8,128)(2,1)}, u32[]{:S(2)}, u32[]{:S(2)}) async-start(bf16[16,64,2048]{2,1,0:T(8,128)(2,1)} %bitcast.179), calls=%async_computation.2 | async-start | bytes 8388608 | tf_op jit(solution)/shard_map/all_to_all | solution.py:126
  292.7 177.1 %reduce-scatter.5.cloned.1.call-start = ((), (), s32[]{:S(2)}) async-start(), calls=%async_computation.11 | async-start | bytes 4456448 | tf_op jit(solution)/shard_map/reduce_scatter | solution.py:135
  371.4 98.4 %copy-start.7 = (bf16[512,128]{1,0:T(8,128)(2,1)S(1)}, bf16[512,128]{1,0:T(8,128)(2,1)}, u32[]{:S(2)}) copy-start(bf16[512,128]{1,0:T(8,128)(2,1)} %add_convert_fusion.1) | copy-start | bytes 393220
  371.4 100.1 %copy-start.25 = (s32[8]{0:T(128)S(1)}, s32[8]{0:T(128)}, u32[]{:S(2)}) copy-start(s32[8]{0:T(128)} %param.33) | copy-start | bytes 100
  371.4 100.1 %copy-start.17 = (s32[8]{0:T(128)S(1)}, s32[8]{0:T(128)}, u32[]{:S(2)}) copy-start(s32[8]{0:T(128)} %param.32) | copy-start | bytes 100
  371.4 111.0 %copy-start.16 = (bf16[2048]{0:T(1024)(128)(2,1)S(1)}, bf16[2048]{0:T(1024)(128)(2,1)}, u32[]{:S(2)}) copy-start(bf16[2048]{0:T(1024)(128)(2,1)} %param.23) | copy-start | bytes 12292
  371.4 111.0 %copy-start.14 = (s32[1,504]{1,0:T(1,128)S(1)}, s32[1,504]{1,0:T(1,128)}, u32[]{:S(2)}) copy-start(s32[1,504]{1,0:T(1,128)} %param.31) | copy-start | bytes 6052
  371.5 175.8 %all-gather.7.cloned.1.call-start = ((), (), s32[]{:S(2)}) async-start(), calls=%async_computation.12 | async-start | bytes 2228224 | tf_op jit(solution)/shard_map/all_gather | solution.py:48
  472.4 77.1 %copy-start.24 = (bf16[2048,64]{0,1:T(8,128)(2,1)S(1)}, bf16[2048,64]{0,1:T(8,128)(2,1)}, u32[]{:S(2)}) copy-start(bf16[2048,64]{0,1:T(8,128)(2,1)} %param.30) | copy-start | bytes 786436
  473.1 109.5 %all-to-all-start.2 = ((s32[16,1,8]{2,1,0:T(1,128)}), s32[16,1,8]{2,1,0:T(1,128)S(1)}, u32[]{:S(2)}, u32[]{:S(2)}) async-start(s32[16,1,8]{2,1,0:T(1,128)} %copy.82), calls=%async_computation.4 | async-start | bytes 16384 | tf_op jit(solution)/shard_map/all_to_all | solution.py:196
  482.2 197.7 %all-gather.9.cloned.1.call-start = ((), (), s32[]{:S(2)}) async-start(), calls=%async_computation.13 | async-start | bytes 1114112 | tf_op jit(solution)/shard_map/all_gather | solution.py:151
  547.2 2.3 copy-start.6
  549.5 1.6 copy-start.22
  579.2 46.9 %copy-start.8 = (bf16[8,64,512]{2,1,0:T(8,128)(2,1)S(1)}, bf16[8,64,512]{2,1,0:T(8,128)(2,1)}, u32[]{:S(2)}) copy-start(bf16[8,64,512]{2,1,0:T(8,128)(2,1)} %param.34) | copy-start | bytes 1572868
  582.6 44.1 %copy-start.23 = (bf16[8,64,512]{2,1,0:T(8,128)(2,1)S(1)}, bf16[8,64,512]{2,1,0:T(8,128)(2,1)}, u32[]{:S(2)}) copy-start(bf16[8,64,512]{2,1,0:T(8,128)(2,1)} %param.35) | copy-start | bytes 1572868
  582.6 43.4 %all-to-all-start.3 = ((bf16[16,8,4096]{2,1,0:T(8,128)(2,1)}), bf16[16,8,4096]{2,1,0:T(8,128)(2,1)S(1)}, u32[]{:S(2)}, u32[]{:S(2)}) async-start(bf16[16,8,4096]{2,1,0:T(8,128)(2,1)} %scatter_fusion.1), calls=%async_computation.5 | async-start | bytes 2097152 | tf_op jit(solution)/shard_map/all_to_all | solution.py:195
  607.8 96.3 %all-gather.11.cloned.1.call-start = ((), (), s32[]{:S(2)}) async-start(), calls=%async_computation.14 | async-start | bytes 2228224 | tf_op jit(solution)/shard_map/all_gather | solution.py:16
  652.7 29.8 %copy-start.9 = (f32[16,8,32]{2,1,0:T(8,128)}, f32[16,8,32]{2,1,0:T(8,128)S(1)}, u32[]{:S(2)}) copy-start(f32[16,8,32]{2,1,0:T(8,128)S(1)} %all_gather.26) | copy-start | bytes 49156
  679.8 2.6 copy-start.10
  686.6 4.3 copy-start.4
  690.8 1.0 copy-start.5
  693.9 14.0 %slice-start = ((f32[16,8,32]{2,1,0:T(8,128)}), f32[15,8,32]{2,1,0:T(8,128)S(1)}, s32[]{:S(2)}) async-start(f32[16,8,32]{2,1,0:T(8,128)} %copy-done.9), calls=%async_computation.15 | async-start | bytes 122880 | tf_op jit(solution)/shard_map/slice | solution.py:18
  693.9 14.1 %slice-start.1 = ((f32[16,8,32]{2,1,0:T(8,128)}), f32[15,8,32]{2,1,0:T(8,128)S(1)}, s32[]{:S(2)}) async-start(f32[16,8,32]{2,1,0:T(8,128)} %copy-done.10), calls=%async_computation.16 | async-start | bytes 122880 | tf_op jit(solution)/shard_map/slice | solution.py:18
  708.0 66.6 %copy-start.1 = (bf16[1,384,2048]{2,1,0:T(8,128)(2,1)S(1)}, bf16[1,384,2048]{2,1,0:T(8,128)(2,1)}, u32[]{:S(2)}) copy-start(bf16[1,384,2048]{2,1,0:T(8,128)(2,1)} %param.28) | copy-start | bytes 4718596
  725.6 23.5 %all-to-all-start.5 = ((f32[16,8,2]{1,2,0:T(2,128)}), f32[16,8,2]{1,2,0:T(2,128)S(1)}, u32[]{:S(2)}, u32[]{:S(2)}) async-start(f32[16,8,2]{1,2,0:T(2,128)} %broadcast_in_dim.100), calls=%async_computation.7 | async-start | bytes 32768 | tf_op jit(solution)/shard_map/all_to_all | solution.py:226
  749.7 11.0 %all-to-all-start.6 = ((f32[16,8,2]{1,2,0:T(2,128)}), f32[16,8,2]{1,2,0:T(2,128)S(1)}, u32[]{:S(2)}, u32[]{:S(2)}) async-start(f32[16,8,2]{1,2,0:T(2,128)} %broadcast_in_dim.101), calls=%async_computation.8 | async-start | bytes 32768 | tf_op jit(solution)/shard_map/all_to_all | solution.py:227
  761.5 11.4 %all-to-all-start.4 = ((f32[16,8,2,128]{3,2,1,0:T(2,128)}), f32[16,8,2,128]{3,2,1,0:T(2,128)S(1)}, u32[]{:S(2)}, u32[]{:S(2)}) async-start(f32[16,8,2,128]{3,2,1,0:T(2,128)} %broadcast_in_dim.99), calls=%async_computation.6 | async-start | bytes 262144 | tf_op jit(solution)/shard_map/all_to_all | solution.py:228
Sparse Core Ops, SparseCore 0:
  11.5 101.9 reduce-scatter.2
  115.7 74.9 all-gather.4
  371.6 98.2 reduce-scatter.4
  472.0 75.2 all-gather.6
  551.1 76.3 all-gather.8
  629.1 74.8 all-gather.10
where the time goes:
time: 783 us; the launch traced here: 781 us
  waiting for transfers between devices  380 us (49%)
  blocking collectives  143 us (18%)
  local copies, waits for them, and re-layouts  97.3 us (12%)
  starting transfers between devices  63.8 us (8%)
  other arithmetic  55.6 us (7%)
  matrix products  26.9 us (3%)
  between operations  14.7 us (2%)
    all_gather x2, waiting for transfers between devices, spread_norm(): gathered = lax.all_gather(hidden, 'col', axis=1, tiled=True)  106 us
    reduce_scatter x1, waiting for transfers between devices, shards(): summed = lax.psum_scatter(projected, 'col', scatter_dimension=1, tiled=True)  102 us
    reduce_scatter x1, waiting for transfers between devices, shards(): lax.psum_scatter(partial_moe, 'col', scatter_dimension=1, tiled=True)  98.3 us
    all_to_all x1, blocking collectives, shards(): lax.all_to_all(outgoing, 'row', split_axis=0, concat_axis=0, tiled=True)  68.1 us
    unnamed x59, local copies, waits for them, and re-layouts  66.1 us
    all_gather x2, blocking collectives, merged_2(): pieces = jax.tree.map(lambda part: lax.all_gather(part, axis), value)  50.6 us
    all_to_all x1, starting transfers between devices, shards(): lax.all_to_all(outbox, 'row', split_axis=0, concat_axis=0, tiled=True)  25.2 us
    all_to_all x1, waiting for transfers between devices, shards(): lax.all_to_all(result.reshape(arrived.shape), 'row', split_axis=0, concat...  24.7 us
  transfers between devices with their start and end apart: 12, of which 10 were waited for; matrix products, arithmetic and copies ran while one was open for 12% of the time, Pallas kernels for 0%

commit v1 on v0

--- a/solution.py
+++ b/solution.py
@@ -45,7 +45,9 @@
 
 
 def spread_norm(hidden, gain_vector):
-    gathered = lax.all_gather(hidden, "col", axis=1, tiled=True)
+    gathered = jnp.concatenate(
+        lax.all_to_all(jnp.stack([hidden] * lax.axis_size("col")), "col", 0, 0), axis=1
+    )
     return (gathered, rms_norm(gathered, gain_vector))
 
 

time: 783 us -> 737 us (0.941)
  waiting for transfers between devices: 380 us -> 329 us
  blocking collectives: 143 us -> 135 us
    all_gather x2 -> x0, waiting for transfers between devices: 106 us -> none  [spread_norm(): gathered = lax.all_gather(hidden, 'col', axis=1, tiled=True)]
    all_to_all x0 -> x2, waiting for transfers between devices: none -> 60.1 us  [spread_norm(): lax.all_to_all(jnp.stack([hidden] * lax.axis_size('col')), 'col', 0, 0)]
    all_to_all x0 -> x2, starting transfers between devices: none -> 14.2 us  [spread_norm(): lax.all_to_all(jnp.stack([hidden] * lax.axis_size('col')), 'col', 0, 0)]
    all_to_all x1, starting transfers between devices: 25.2 us -> 14.1 us  [shards(): lax.all_to_all(outbox, 'row', split_axis=0, concat_axis=0, tiled=True)]
    unnamed x59 -> x53, local copies, waits for them, and re-layouts: 66.1 us -> 67.3 us
  transfers between devices with their start and end apart: 12 -> 12, of which waited for: 10 -> 10; matrix products, arithmetic and copies ran while one was open for 12% -> 13% of each run, Pallas kernels for 0% -> 0%
where the time goes in v1:
time: 737 us; the launch traced here: 735 us
  waiting for transfers between devices  329 us (45%)
  blocking collectives  135 us (18%)
  local copies, waits for them, and re-layouts  102 us (14%)
  starting transfers between devices  69 us (9%)
  other arithmetic  57.8 us (8%)
  matrix products  28.3 us (4%)
  between operations  14.4 us (2%)
    reduce_scatter x1, waiting for transfers between devices, shards(): summed = lax.psum_scatter(projected, 'col', scatter_dimension=1, tiled=True)  102 us
    reduce_scatter x1, waiting for transfers between devices, shards(): lax.psum_scatter(partial_moe, 'col', scatter_dimension=1, tiled=True)  95.6 us
    unnamed x53, local copies, waits for them, and re-layouts  67.3 us
    all_to_all x1, blocking collectives, shards(): lax.all_to_all(outgoing, 'row', split_axis=0, concat_axis=0, tiled=True)  60.9 us
    all_to_all x2, waiting for transfers between devices, spread_norm(): lax.all_to_all(jnp.stack([hidden] * lax.axis_size('col')), 'col', 0, 0)  60.1 us
    all_gather x2, blocking collectives, merged_2(): pieces = jax.tree.map(lambda part: lax.all_gather(part, axis), value)  50.2 us
    all_to_all x1, waiting for transfers between devices, shards(): lax.all_to_all(result.reshape(arrived.shape), 'row', split_axis=0, concat...  24.7 us
    all_gather x1, blocking collectives, shards(): lax.all_gather(dec_query, 'col', axis=1, tiled=True)  23.5 us
  transfers between devices with their start and end apart: 12, of which 10 were waited for; matrix products, arithmetic and copies ran while one was open for 13% of the time, Pallas kernels for 0%

profile of v1, /device:TPU:1, one launch (start us, length us, event | category | flops | bytes accessed | tf_op | source)
XLA Modules:
  0.0 735.5 jit_solution(9118210504465858847)
XLA Ops:
  7.2 4.1 fusion.100
  11.3 102.1 %reduce-scatter.3.cloned.1.call-done = f32[512,128]{1,0:T(8,128)} async-done(((f32[512,2048]{1,0:T(8,128)}), f32[512,128]{1,0:T(8,128)}) %reduce-scatter.3.cloned.1.call-update) | async-done | bytes 262160 | tf_op jit(solution)/shard_map/reduce_scatter | solution.py:89
  114.4 1.7 stack.6
  116.1 7.1 all-to-all-start
  125.5 30.4 %scatter_custom_fusion.3 = s32[1024]{0:T(1024)S(1)} fusion(s32[8192]{0:T(1024)S(1)} %reshape.367, s32[8192]{0:T(1024)S(1)} %reshape.369, s32[]{:T(128)} %constant.121.clone.1), kind=kCustom, calls=%fused_computation.150 | custom fusion | bytes 4100
  156.1 15.2 %all-to-all-done = bf16[16,512,128]{2,1,0:T(8,128)(2,1)} async-done(((bf16[16,512,128]{2,1,0:T(8,128)(2,1)}), bf16[16,512,128]{2,1,0:T(8,128)(2,1)}, u32[]{:S(2)}, u32[]{:S(2)}) %all-to-all-start) | async-done | bytes 2097184 | tf_op jit(solution)/shard_map/all_to_all | solution.py:49
  171.3 2.1 fusion.4
  173.4 2.1 fusion.6
  175.5 1.5 concatenate.52
  177.0 10.7 %gather_fusion = bf16[1024,2048]{1,0:T(8,128)(2,1)} fusion(bf16[513,2048]{1,0:T(8,128)(2,1)} %concatenate.52, s32[1024]{0:T(1024)S(1)} %broadcast_clamp_fusion), kind=kCustom, calls=%fused_computation | custom fusion | bytes 8392704 | tf_op jit(solution)/shard_map/gather | solution.py:118
  187.7 60.9 %all_to_all.49 = bf16[16,64,2048]{2,1,0:T(8,128)(2,1)S(1)} all-to-all(bf16[16,64,2048]{2,1,0:T(8,128)(2,1)} %bitcast.197), channel_id=1, replica_groups=mesh['row'=16,'col'=16] {'row'}, dimensions={0} | all-to-all | bytes 8388608 | tf_op jit(solution)/shard_map/all_to_all | solution.py:122
  248.6 2.0 copy-done.3
  250.6 3.6 fusion.15
  254.1 9.6 %convolution_convert_fusion = bf16[1024,2048]{1,0:T(8,128)(2,1)} fusion(bf16[1,384,2048]{2,1,0:T(8,128)(2,1)S(1)} %copy-done, f32[1024,384]{1,0:T(8,128)} %fusion.15, bf16[1024,2048]{1,0:T(8,128)(2,1)} %bitcast.201, bf16[1,2048,384]{2,1,0:T(8,128)(2,1)} %param.27), kind=kOutput, calls=%fused_computation.29 | convolution fusion | flops 3225681920 | bytes 13107200 | tf_op jit(solution)/shard_map/dot_general | solution.py:127
  263.7 5.5 all-to-all-start.2
  269.8 30.4 %scatter_custom_fusion.4 = f32[1024]{0:T(1024)S(1)} fusion(s32[8192]{0:T(1024)S(1)} %reshape.367, f32[8192]{0:T(1024)S(1)} %reshape.375, f32[]{:T(128)} %constant.120.clone.1), kind=kCustom, calls=%fused_computation.148 | custom fusion | bytes 4100
  300.3 24.7 %all-to-all-done.2 = bf16[16,64,2048]{2,1,0:T(8,128)(2,1)} async-done(((bf16[16,64,2048]{2,1,0:T(8,128)(2,1)}), bf16[16,64,2048]{2,1,0:T(8,128)(2,1)}, u32[]{:S(2)}, u32[]{:S(2)}) %all-to-all-start.2) | async-done | bytes 4194336 | tf_op jit(solution)/shard_map/all_to_all | solution.py:128
  324.9 6.0 convert_multiply_fusion
  331.0 16.9 %scatter_custom_fusion = f32[512,2048]{1,0:T(8,128)} fusion(s32[1024]{0:T(1024)S(1)} %bitcast.211, f32[1024,2048]{1,0:T(8,128)} %bitcast.198, f32[]{:T(128)} %constant.120.clone.1), kind=kCustom, calls=%fused_computation.30 | custom fusion | flops 2097152 | bytes 4194816 | tf_op jit(solution)/shard_map/scatter-add | solution.py:135
  347.9 95.6 %reduce-scatter.5.cloned.1.call-done = f32[512,128]{1,0:T(8,128)} async-done(((f32[512,2048]{1,0:T(8,128)}), f32[512,128]{1,0:T(8,128)}) %reduce-scatter.5.cloned.1.call-update) | async-done | bytes 262160 | tf_op jit(solution)/shard_map/reduce_scatter | solution.py:137
  444.6 1.5 stack.7
  446.1 7.0 all-to-all-start.3
  456.3 44.9 %all-to-all-done.3 = bf16[16,512,128]{1,2,0:T(8,128)(2,1)} async-done(((bf16[16,512,128]{1,2,0:T(8,128)(2,1)}), bf16[16,512,128]{1,2,0:T(8,128)(2,1)}, u32[]{:S(2)}, u32[]{:S(2)}) %all-to-all-start.3) | async-done | bytes 2097184 | tf_op jit(solution)/shard_map/all_to_all | solution.py:49
  501.2 9.9 %all-to-all-start.4 = ((s32[16,1,8]{2,1,0:T(1,128)}), s32[16,1,8]{2,1,0:T(1,128)S(1)}, u32[]{:S(2)}, u32[]{:S(2)}) async-start(s32[16,1,8]{2,1,0:T(1,128)} %copy.87), calls=%async_computation.6 | async-start | bytes 16384 | tf_op jit(solution)/shard_map/all_to_all | solution.py:198
  511.3 2.1 multiply_reduce_fusion
  513.4 2.2 fusion.8
  515.6 1.3 copy-done.2
  518.1 2.6 convolution_convert_fusion.1
  521.3 23.5 %all_gather.16 = bf16[8,4096]{1,0:T(8,128)(2,1)S(1)} all-gather(bf16[8,256]{1,0:T(8,128)(2,1)S(1)} %get-tuple-element.84), channel_id=1, replica_groups=mesh['row'=16,'col'=16] {'col'}, dimensions={1}, use_global_device_ids=true | all-gather | bytes 69632 | tf_op jit(solution)/shard_map/all_gather | solution.py:154
  545.9 3.3 scatter_fusion.1
  549.3 14.1 %all-to-all-start.5 = ((bf16[16,8,4096]{2,1,0:T(8,128)(2,1)}), bf16[16,8,4096]{2,1,0:T(8,128)(2,1)S(1)}, u32[]{:S(2)}, u32[]{:S(2)}) async-start(bf16[16,8,4096]{2,1,0:T(8,128)(2,1)} %scatter_fusion.1), calls=%async_computation.7 | async-start | bytes 2097152 | tf_op jit(solution)/shard_map/all_to_all | solution.py:197
  563.5 18.9 %all-to-all-done.5 = bf16[16,8,4096]{2,1,0:T(8,128)(2,1)S(1)} async-done(((bf16[16,8,4096]{2,1,0:T(8,128)(2,1)}), bf16[16,8,4096]{2,1,0:T(8,128)(2,1)S(1)}, u32[]{:S(2)}, u32[]{:S(2)}) %all-to-all-start.5) | async-done | bytes 1048608 | tf_op jit(solution)/shard_map/all_to_all | solution.py:197
  583.0 1.2 convolution_bitcast_fusion
  585.6 23.9 %all_gather.18 = f32[16,8,32]{2,1,0:T(8,128)S(1)} all-gather(f32[1,8,32]{2,1,0:T(8,128)S(1)} %all_gather_reshape.10), channel_id=1, replica_groups=mesh['row'=16,'col'=16] {'col'}, dimensions={0}, use_global_device_ids=true | all-gather | bytes 17408 | tf_op jit(solution)/shard_map/all_gather | solution.py:16
  609.6 26.2 %all_gather.17 = f32[16,8,32]{2,1,0:T(8,128)S(1)} all-gather(f32[1,8,32]{2,1,0:T(8,128)S(1)} %all_gather_reshape.9), channel_id=1, replica_groups=mesh['row'=16,'col'=16] {'col'}, dimensions={0}, use_global_device_ids=true | all-gather | bytes 17408 | tf_op jit(solution)/shard_map/all_gather | solution.py:16
  635.8 1.3 fusion.94
  638.5 1.4 fusion.93
  640.0 2.5 fusion.96
  642.5 3.1 fusion.19
  649.9 7.3 all-gather.5.cloned.1.call-done
  657.2 3.0 slice.119
  661.1 16.8 %while.14 = (s32[]{:T(128)}, f32[8,32]{1,0:T(8,128)S(1)}, f32[8,32]{1,0:T(8,128)S(1)}, f32[8,32,128]{2,1,0:T(8,128)S(1)}, f32[15,8,32]{2,1,0:T(8,128)S(1)}, /*in...) while((s32[]{:T(128)}, f32[8,32]{1,0:T(8,128)S(1)}, f32[8,32]{1,0:T(8,128)S(1)}, ...), condition=%wide.region_20.21_spmd, body=%wide.region_19.20_spmd.sunk | while | flops 99842 | bytes 403549 | solution.py:19
  678.7 17.4 %all-to-all-start.7 = ((f32[16,8,2]{1,2,0:T(2,128)}), f32[16,8,2]{1,2,0:T(2,128)S(1)}, u32[]{:S(2)}, u32[]{:S(2)}) async-start(f32[16,8,2]{1,2,0:T(2,128)} %broadcast_in_dim.100), calls=%async_computation.9 | async-start | bytes 32768 | tf_op jit(solution)/shard_map/all_to_all | solution.py:228
  696.3 7.1 all-to-all-done.7
  704.0 3.7 all-to-all-start.8
  708.5 6.6 all-to-all-done.8
  715.8 3.7 all-to-all-start.6
  720.2 6.9 all-to-all-done.6
  (181 shorter events, 41.8 us)
Async XLA Ops:
  7.2 246.9 %copy-start = (bf16[1,384,2048]{2,1,0:T(8,128)(2,1)S(1)}, bf16[1,384,2048]{2,1,0:T(8,128)(2,1)}, u32[]{:S(2)}) copy-start(bf16[1,384,2048]{2,1,0:T(8,128)(2,1)} %param.28) | copy-start | bytes 4718596
  7.2 106.3 %reduce-scatter.3.cloned.1.call-start = ((), (), s32[]{:S(2)}) async-start(), calls=%async_computation.11 | async-start | bytes 4456448 | tf_op jit(solution)/shard_map/reduce_scatter | solution.py:89
  11.3 102.2 %copy-start.11 = (bf16[512,128]{1,0:T(8,128)(2,1)S(1)}, bf16[512,128]{1,0:T(8,128)(2,1)}, u32[]{:S(2)}) copy-start(bf16[512,128]{1,0:T(8,128)(2,1)} %param.20) | copy-start | bytes 393220
  116.1 7.1 copy-start.12
  116.1 8.8 %copy-start.19 = (s32[2]{0:T(128)S(1)}, s32[2]{0:T(128)}, u32[]{:S(2)}) copy-start(s32[2]{0:T(128)} %constant.155) | copy-start | bytes 28
  116.1 8.9 %copy-start.18 = (s32[2]{0:T(128)S(1)}, s32[2]{0:T(128)}, u32[]{:S(2)}) copy-start(s32[2]{0:T(128)} %constant.158) | copy-start | bytes 28
  116.1 40.0 %copy-start.15 = (bf16[2048]{0:T(1024)(128)(2,1)S(1)}, bf16[2048]{0:T(1024)(128)(2,1)}, u32[]{:S(2)}) copy-start(bf16[2048]{0:T(1024)(128)(2,1)} %param.22) | copy-start | bytes 12292
  116.1 55.1 %all-to-all-start = ((bf16[16,512,128]{2,1,0:T(8,128)(2,1)}), bf16[16,512,128]{2,1,0:T(8,128)(2,1)}, u32[]{:S(2)}, u32[]{:S(2)}) async-start(bf16[16,512,128]{2,1,0:T(8,128)(2,1)} %stack.6), calls=%async_computation.1 | async-start | bytes 4194304 | tf_op jit(solution)/shard_map/all_to_all | solution.py:49
  187.7 62.9 %copy-start.20 = (bf16[1,2048,384]{2,1,0:T(8,128)(2,1)S(1)}, bf16[1,2048,384]{2,1,0:T(8,128)(2,1)}, u32[]{:S(2)}) copy-start(bf16[1,2048,384]{2,1,0:T(8,128)(2,1)} %param.26) | copy-start | bytes 4718596
  248.6 2.0 copy-start.3
  263.7 5.7 copy-start.13
  263.7 61.3 %all-to-all-start.2 = ((bf16[16,64,2048]{2,1,0:T(8,128)(2,1)}), bf16[16,64,2048]{2,1,0:T(8,128)(2,1)}, u32[]{:S(2)}, u32[]{:S(2)}) async-start(bf16[16,64,2048]{2,1,0:T(8,128)(2,1)} %bitcast.199), calls=%async_computation.3 | async-start | bytes 8388608 | tf_op jit(solution)/shard_map/all_to_all | solution.py:128
  269.1 174.4 %reduce-scatter.5.cloned.1.call-start = ((), (), s32[]{:S(2)}) async-start(), calls=%async_computation.12 | async-start | bytes 4456448 | tf_op jit(solution)/shard_map/reduce_scatter | solution.py:137
  444.5 1.6 copy-start.7
  446.1 7.1 copy-start.16
  446.1 7.1 copy-start.22
  446.1 7.1 copy-start.17
  446.1 8.7 %copy-start.14 = (s32[1,504]{1,0:T(1,128)S(1)}, s32[1,504]{1,0:T(1,128)}, u32[]{:S(2)}) copy-start(s32[1,504]{1,0:T(1,128)} %param.31) | copy-start | bytes 6052
  446.1 55.0 %all-to-all-start.3 = ((bf16[16,512,128]{1,2,0:T(8,128)(2,1)}), bf16[16,512,128]{1,2,0:T(8,128)(2,1)}, u32[]{:S(2)}, u32[]{:S(2)}) async-start(bf16[16,512,128]{1,2,0:T(8,128)(2,1)} %stack.7), calls=%async_computation.5 | async-start | bytes 4194304 | tf_op jit(solution)/shard_map/all_to_all | solution.py:49
  501.2 48.1 %all-to-all-start.4 = ((s32[16,1,8]{2,1,0:T(1,128)}), s32[16,1,8]{2,1,0:T(1,128)S(1)}, u32[]{:S(2)}, u32[]{:S(2)}) async-start(s32[16,1,8]{2,1,0:T(1,128)} %copy.87), calls=%async_computation.6 | async-start | bytes 16384 | tf_op jit(solution)/shard_map/all_to_all | solution.py:198
  511.1 124.8 %all-gather.3.cloned.1.call-start = ((), (), s32[]{:S(2)}) async-start(), calls=%async_computation.13 | async-start | bytes 1114112 | tf_op jit(solution)/shard_map/all_gather | solution.py:153
  513.4 3.5 copy-start.8
  515.6 1.4 copy-start.2
  545.9 36.6 %copy-start.6 = (bf16[8,64,512]{2,1,0:T(8,128)(2,1)S(1)}, bf16[8,64,512]{2,1,0:T(8,128)(2,1)}, u32[]{:S(2)}) copy-start(bf16[8,64,512]{2,1,0:T(8,128)(2,1)} %param.34) | copy-start | bytes 1572868
  549.2 33.8 %copy-start.21 = (bf16[8,64,512]{2,1,0:T(8,128)(2,1)S(1)}, bf16[8,64,512]{2,1,0:T(8,128)(2,1)}, u32[]{:S(2)}) copy-start(bf16[8,64,512]{2,1,0:T(8,128)(2,1)} %param.35) | copy-start | bytes 1572868
  549.3 33.2 %all-to-all-start.5 = ((bf16[16,8,4096]{2,1,0:T(8,128)(2,1)}), bf16[16,8,4096]{2,1,0:T(8,128)(2,1)S(1)}, u32[]{:S(2)}, u32[]{:S(2)}) async-start(bf16[16,8,4096]{2,1,0:T(8,128)(2,1)} %scatter_fusion.1), calls=%async_computation.7 | async-start | bytes 2097152 | tf_op jit(solution)/shard_map/all_to_all | solution.py:197
  563.4 93.8 %all-gather.5.cloned.1.call-start = ((), (), s32[]{:S(2)}) async-start(), calls=%async_computation.14 | async-start | bytes 2228224 | tf_op jit(solution)/shard_map/all_gather | solution.py:16
  609.6 28.8 %copy-start.9 = (f32[16,8,32]{2,1,0:T(8,128)}, f32[16,8,32]{2,1,0:T(8,128)S(1)}, u32[]{:S(2)}) copy-start(f32[16,8,32]{2,1,0:T(8,128)S(1)} %all_gather.18) | copy-start | bytes 49156
  635.8 2.6 copy-start.10
  642.5 4.3 copy-start.4
  646.8 1.0 copy-start.5
  649.9 11.2 %slice-start = ((f32[16,8,32]{2,1,0:T(8,128)}), f32[15,8,32]{2,1,0:T(8,128)S(1)}, s32[]{:S(2)}) async-start(f32[16,8,32]{2,1,0:T(8,128)} %copy-done.9), calls=%async_computation.15 | async-start | bytes 122880 | tf_op jit(solution)/shard_map/slice | solution.py:18
  649.9 11.2 %slice-start.1 = ((f32[16,8,32]{2,1,0:T(8,128)}), f32[15,8,32]{2,1,0:T(8,128)S(1)}, s32[]{:S(2)}) async-start(f32[16,8,32]{2,1,0:T(8,128)} %copy-done.10), calls=%async_computation.16 | async-start | bytes 122880 | tf_op jit(solution)/shard_map/slice | solution.py:18
  661.1 67.8 %copy-start.1 = (bf16[1,384,2048]{2,1,0:T(8,128)(2,1)S(1)}, bf16[1,384,2048]{2,1,0:T(8,128)(2,1)}, u32[]{:S(2)}) copy-start(bf16[1,384,2048]{2,1,0:T(8,128)(2,1)} %param.28) | copy-start | bytes 4718596
  678.7 24.7 %all-to-all-start.7 = ((f32[16,8,2]{1,2,0:T(2,128)}), f32[16,8,2]{1,2,0:T(2,128)S(1)}, u32[]{:S(2)}, u32[]{:S(2)}) async-start(f32[16,8,2]{1,2,0:T(2,128)} %broadcast_in_dim.100), calls=%async_computation.9 | async-start | bytes 32768 | tf_op jit(solution)/shard_map/all_to_all | solution.py:228
  704.0 11.0 %all-to-all-start.8 = ((f32[16,8,2]{1,2,0:T(2,128)}), f32[16,8,2]{1,2,0:T(2,128)S(1)}, u32[]{:S(2)}, u32[]{:S(2)}) async-start(f32[16,8,2]{1,2,0:T(2,128)} %broadcast_in_dim.101), calls=%async_computation.10 | async-start | bytes 32768 | tf_op jit(solution)/shard_map/all_to_all | solution.py:229
  715.8 11.4 %all-to-all-start.6 = ((f32[16,8,2,128]{3,2,1,0:T(2,128)}), f32[16,8,2,128]{3,2,1,0:T(2,128)S(1)}, u32[]{:S(2)}, u32[]{:S(2)}) async-start(f32[16,8,2,128]{3,2,1,0:T(2,128)} %broadcast_in_dim.99), calls=%async_computation.8 | async-start | bytes 262144 | tf_op jit(solution)/shard_map/all_to_all | solution.py:230
Sparse Core Ops, SparseCore 0:
  11.4 101.9 reduce-scatter.2
  348.0 95.4 reduce-scatter.4
  518.2 64.8 all-gather.2
  584.8 72.2 all-gather.4
